TPU v7x, 128 devices: a whole 4x4x4 slice. The times are simulated.
128 devices in a mesh: row: 8 (over z, core), col: 16 (over y, x).
Axes of the slice: x: 4, y: 4, z: 4, core: 2. Of those that a mesh axis runs over, the one named last changes fastest.
Arguments:
- kernel: float32 [16384, 16384], P('row', 'col'), may hold values from 0 to 3, as said below
Outputs:
- trailing: float32 [16384, 16384], P('row', 'col')
- factor_t: float32 [1024, 16384], P('col', 'row')
Inputs may be any that keep to these rules, and one draw needn't show every extreme that they name: K is symmetric: an RBF kernel over 256 donor features plus each donor's noise variance, of 0.5 or more, on the diagonal.
All inputs are finite; a program needn't handle non-finite values.
Results may differ from a plain program's by a relative error of at most 0.0003.
Values sent between devices are 32-bit elements; how exact they have to be, the bound alone decides.
A program may use at most 128 MiB of HBM per device.

v0:
```python
import jax
import jax.numpy as jnp
from jax import lax
from jax.sharding import PartitionSpec as P

PANEL = 512
PANELS = 2
TILE = 32
HIGHEST = lax.Precision.HIGHEST


def mm(a, b):
    return jnp.dot(a, b, precision=HIGHEST, preferred_element_type=jnp.float32)


def mm_tn(a, b):
    return lax.dot_general(
        a, b, (((0,), (0,)), ((), ())), precision=HIGHEST, preferred_element_type=jnp.float32
    )


def mm_nt(a, b):
    return lax.dot_general(
        a, b, (((1,), (1,)), ((), ())), precision=HIGHEST, preferred_element_type=jnp.float32
    )


def tri_inverse(lower):
    eye = jnp.eye(lower.shape[0], dtype=lower.dtype)
    return jax.scipy.linalg.solve_triangular(lower, eye, lower=True)


def sym_chol(block):
    return jnp.linalg.cholesky(block)


def local(kernel):
    grid_rows = lax.axis_size("row")
    grid_cols = lax.axis_size("col")
    my_row = lax.axis_index("row")
    my_col = lax.axis_index("col")
    rows_loc, cols_loc = kernel.shape
    lead = PANELS * PANEL
    lead_rt = lead // (TILE * grid_rows)
    lead_ct = lead // (TILE * grid_cols)
    lead_r = lead_rt * TILE
    lead_c = lead_ct * TILE
    row_local = jnp.arange(rows_loc, dtype=jnp.int32)
    row_ids = (row_local // TILE * grid_rows + my_row) * TILE + row_local % TILE
    col_local = jnp.arange(cols_loc, dtype=jnp.int32)
    col_ids = (col_local // TILE * grid_cols + my_col) * TILE + col_local % TILE
    corner = kernel[:lead_r, :lead_c].reshape(1, lead_r * lead_c)
    blocks = lax.all_gather(corner, ("row", "col"), axis=0, tiled=True)
    blocks = blocks.reshape(grid_rows, grid_cols, lead_rt, TILE, lead_ct, TILE)
    a_lead = blocks.transpose(2, 0, 3, 4, 1, 5).reshape(lead, lead)
    cols_part = lax.all_gather(kernel[:, :lead_c], "col", axis=1, tiled=True)
    cols_part = cols_part.reshape(rows_loc, grid_cols, lead_ct, TILE)
    x_rows = cols_part.transpose(0, 2, 1, 3).reshape(rows_loc, lead)
    rows_part = lax.all_gather(kernel[:lead_r, :], "row", axis=0, tiled=True)
    rows_part = rows_part.reshape(grid_rows, lead_rt, TILE, cols_loc)
    y_cols = rows_part.transpose(1, 0, 2, 3).reshape(lead, cols_loc)
    a00 = a_lead[:PANEL, :PANEL]
    a01 = a_lead[:PANEL, PANEL:]
    a11 = a_lead[PANEL:, PANEL:]
    l0 = sym_chol(a00)
    l0inv = tri_inverse(l0)
    g0p1 = mm(l0inv, a01)
    s11 = a11 - mm_tn(g0p1, g0p1)
    l1 = sym_chol(s11)
    l1inv = tri_inverse(l1)

    def factor(panel_t, ids):
        g0 = mm(l0inv, panel_t[:PANEL])
        s1 = panel_t[PANEL:] - mm_tn(g0p1, g0)
        g1 = mm(l1inv, s1)
        g1 = jnp.where(ids[None, :] >= PANEL, g1, 0.0)
        return jnp.concatenate([g0, g1], axis=0)

    g_rows = factor(x_rows.T, row_ids)
    g_cols = factor(y_cols, col_ids)
    schur = kernel - mm_tn(g_rows, g_cols)
    keep = (row_ids[:, None] >= lead) & (col_ids[None, :] >= lead)
    trailing = jnp.where(keep, schur, 0.0)
    per_col = lead // grid_cols
    factor_out = lax.dynamic_slice_in_dim(g_rows, my_col * per_col, per_col, 0)
    return (trailing, factor_out)


def solution(mesh):
    return jax.shard_map(
        local,
        mesh=mesh,
        in_specs=(P("row", "col"),),
        out_specs=(P("row", "col"), P("col", "row")),
        check_vma=False,
    )
```

profile of v0, /device:TPU:1, one launch (start us, length us, event | category | flops | bytes accessed | tf_op | source)
XLA Modules:
  0.0 584.9 jit_solution(12073595241916444088)
XLA Ops:
  12.2 34.1 %all-gather.7.cloned.1.call-done = f32[1024,1024]{1,0:T(8,128)} async-done(((f32[128,1024]{1,0:T(8,128)}), f32[1024,1024]{1,0:T(8,128)}) %all-gather.7.cloned.1.call-update) | async-done | bytes 4194320 | tf_op jit(solution)/shard_map/all_gather | solution.py:59
  51.7 65.0 %all-gather.9.cloned.1.call-done = f32[128,1,8192]{2,1,0:T(1,128)} async-done(((f32[1,1,8192]{2,1,0:T(1,128)}), f32[128,1,8192]{2,1,0:T(1,128)}) %all-gather.9.cloned.1.call-update) | async-done | bytes 4194320 | tf_op jit(solution)/shard_map/all_gather | solution.py:53
  116.7 13.2 %reduce.16 = f32[128,8192]{1,0:T(8,128)} reduce(f32[128,1,8192]{2,1,0:T(1,128)} %all-gather.9.cloned.1.call-done, f32[]{:T(128)} %constant.211), dimensions={1}, to_apply=%all-gather.reduce_sub_computation | reduce | bytes 8388612 | tf_op jit(solution)/shard_map/all_gather | solution.py:53
  129.9 16.6 %reshape.139 = f32[8,16,4,32,2,32]{5,4,3,2,1,0:T(2,128)} reshape(f32[128,8192]{1,0:T(8,128)} %reduce.16) | data formatting | bytes 8388608 | tf_op jit(solution)/shard_map/reshape | solution.py:54
  146.5 26.1 %copy.20 = f32[4,8,32,2,16,32]{2,1,0,5,4,3:T(8,128)} copy(f32[4,8,32,2,16,32]{5,3,2,0,4,1:T(2,128)} %bitcast.121) | data formatting | bytes 8388608 | tf_op jit(solution)/shard_map/transpose | solution.py:55
  172.6 14.3 %reshape.140 = f32[1024,1024]{0,1:T(8,128)} reshape(f32[4,8,32,2,16,32]{2,1,0,5,4,3:T(8,128)} %copy.20) | data formatting | bytes 8388608 | tf_op jit(solution)/shard_map/reshape | solution.py:55
  193.2 11.7 %cholesky.286 = f32[128,128]{1,0:T(8,128)S(1)} custom-call(f32[128,128]{1,0:T(8,128)S(1)} %cholesky.426), custom_call_target="Cholesky" | custom-call | tf_op jit(solution)/shard_map/jit(cholesky)/cholesky | solution.py:34
  204.9 9.8 %custom-call.27 = f32[1,128,128]{1,2,0:T(8,128)S(1)} custom-call(f32[1,128,128]{2,1,0:T(8,128)S(1)} %get-tuple-element.61), custom_call_target="InvertDiagBlocksLowerTriangular" | custom-call | tf_op jit(solution)/shard_map/jit(cholesky)/cholesky | solution.py:34
  217.4 11.7 %cholesky.305 = f32[128,128]{1,0:T(8,128)S(1)} custom-call(f32[128,128]{1,0:T(8,128)S(1)} %cholesky.430), custom_call_target="Cholesky" | custom-call | tf_op jit(solution)/shard_map/jit(cholesky)/cholesky | solution.py:34
  229.1 10.0 %custom-call.28 = f32[1,128,128]{1,2,0:T(8,128)S(1)} custom-call(f32[1,128,128]{2,1,0:T(8,128)S(1)} %get-tuple-element.58), custom_call_target="InvertDiagBlocksLowerTriangular" | custom-call | tf_op jit(solution)/shard_map/jit(cholesky)/cholesky | solution.py:34
  240.7 11.7 %cholesky.326 = f32[128,128]{1,0:T(8,128)S(1)} custom-call(f32[128,128]{1,0:T(8,128)S(1)} %cholesky.435), custom_call_target="Cholesky" | custom-call | tf_op jit(solution)/shard_map/jit(cholesky)/cholesky | solution.py:34
  252.4 9.8 %custom-call.29 = f32[1,128,128]{1,2,0:T(8,128)S(1)} custom-call(f32[1,128,128]{2,1,0:T(8,128)S(1)} %get-tuple-element.55), custom_call_target="InvertDiagBlocksLowerTriangular" | custom-call | tf_op jit(solution)/shard_map/jit(cholesky)/cholesky | solution.py:34
  263.7 11.7 %cholesky.343 = f32[128,128]{1,0:T(8,128)S(1)} custom-call(f32[128,128]{1,0:T(8,128)S(1)} %convolution_subtract_fusion.12), custom_call_target="Cholesky" | custom-call | tf_op jit(solution)/shard_map/jit(cholesky)/cholesky | solution.py:34
  281.6 12.0 %while.4 = (s32[]{:T(128)}, f32[512,512]{1,0:T(8,128)}, s32[4,2]{0,1:T(2,128)S(1)}, f32[4,128,128]{2,1,0:T(8,128)S(1)}, s32[]{:T(128)}) while((s32[]{:T(128)}, f32[512,512]{1,0:T(8,128)}, s32[4,2]{0,1:T(2,128)S(1)}, f32[4,128,128]{2,1,0:T(8,128)S(1)}, s32[]{:T(128)}) %tuple.58), condition=%wide.while_cond, body=%wide.while_body.sunk | while | flops 2 | bytes 131181 | solution.py:30
  293.7 39.3 %custom-call.30 = f32[4,128,128]{1,2,0:T(8,128)S(1)} custom-call(f32[4,128,128]{2,1,0:T(8,128)S(1)} %get-tuple-element.18), custom_call_target="InvertDiagBlocksLowerTriangular" | custom-call | tf_op jit(solution)/shard_map/jit(_solve_triangular)/triangular_solve | solution.py:30
  349.1 11.7 %cholesky.358 = f32[128,128]{1,0:T(8,128)S(1)} custom-call(f32[128,128]{1,0:T(8,128)S(1)} %cholesky.439), custom_call_target="Cholesky" | custom-call | tf_op jit(solution)/shard_map/jit(cholesky)/cholesky | solution.py:34
  362.0 10.0 %custom-call.31 = f32[1,128,128]{1,2,0:T(8,128)S(1)} custom-call(f32[1,128,128]{2,1,0:T(8,128)S(1)} %get-tuple-element.51), custom_call_target="InvertDiagBlocksLowerTriangular" | custom-call | tf_op jit(solution)/shard_map/jit(cholesky)/cholesky | solution.py:34
  375.1 11.7 %cholesky.377 = f32[128,128]{1,0:T(8,128)S(1)} custom-call(f32[128,128]{1,0:T(8,128)S(1)} %cholesky.443), custom_call_target="Cholesky" | custom-call | tf_op jit(solution)/shard_map/jit(cholesky)/cholesky | solution.py:34
  399.7 11.7 %cholesky.398 = f32[128,128]{1,0:T(8,128)S(1)} custom-call(f32[128,128]{1,0:T(8,128)S(1)} %cholesky.448), custom_call_target="Cholesky" | custom-call | tf_op jit(solution)/shard_map/jit(cholesky)/cholesky | solution.py:34
  412.0 10.0 %custom-call.33 = f32[1,128,128]{1,2,0:T(8,128)S(1)} custom-call(f32[1,128,128]{2,1,0:T(8,128)S(1)} %get-tuple-element.45), custom_call_target="InvertDiagBlocksLowerTriangular" | custom-call | tf_op jit(solution)/shard_map/jit(cholesky)/cholesky | solution.py:34
  424.3 11.7 %cholesky.415 = f32[128,128]{1,0:T(8,128)S(1)} custom-call(f32[128,128]{1,0:T(8,128)S(1)} %convolution_subtract_fusion.11), custom_call_target="Cholesky" | custom-call | tf_op jit(solution)/shard_map/jit(cholesky)/cholesky | solution.py:34
  444.4 11.7 %while.5 = (s32[]{:T(128)}, f32[512,512]{1,0:T(8,128)}, s32[4,2]{0,1:T(2,128)S(1)}, f32[4,128,128]{2,1,0:T(8,128)S(1)}, s32[]{:T(128)}) while((s32[]{:T(128)}, f32[512,512]{1,0:T(8,128)}, s32[4,2]{0,1:T(2,128)S(1)}, f32[4,128,128]{2,1,0:T(8,128)S(1)}, s32[]{:T(128)}) %tuple.70), condition=%wide.while_cond.clone, body=%wide.while_body.clone.sunk | while | flops 2 | bytes 131181 | solution.py:30
  456.1 39.7 %custom-call.34 = f32[4,128,128]{1,2,0:T(8,128)S(1)} custom-call(f32[4,128,128]{2,1,0:T(8,128)S(1)} %get-tuple-element.19), custom_call_target="InvertDiagBlocksLowerTriangular" | custom-call | tf_op jit(solution)/shard_map/jit(_solve_triangular)/triangular_solve | solution.py:30
  546.5 31.7 %subtract_select_fusion = f32[2048,1024]{1,0:T(8,128)} fusion(f32[2048,1024]{1,0:T(8,128)} %param.4, pred[1024]{0:T(1024)(128)(4,1)S(1)} %get-tuple-element.67, pred[2048]{0:T(1024)(128)(4,1)S(1)} %get-tuple-element.69, f32[512,1024]{1,0:T(8,128)S(1)} %copy-done.11, f32[512,1024]{1,0:T(8,128)S(1)} %copy-done.3, f32[512,2048]{1,0:T(8,128)S(1)} %fusion.7, ...), kind=kOutput, calls=%fused_computation.8 | convolution fusion | flops 25779240960 | bytes 29363200 | tf_op jit(solution)/shard_map/dot_general | solution.py:17
  (140 shorter events, 141.8 us)
Async XLA Ops:
  7.2 3.7 slice-start
  7.2 39.1 %all-gather.7.cloned.1.call-start = ((), (), s32[]{:S(2)}) async-start(), calls=%async_computation.1 | async-start | bytes 4718592 | tf_op jit(solution)/shard_map/all_gather | solution.py:59
  9.2 107.5 %all-gather.9.cloned.1.call-start = ((), (), s32[]{:S(2)}) async-start(), calls=%async_computation.2 | async-start | bytes 4227072 | tf_op jit(solution)/shard_map/all_gather | solution.py:53
  10.8 507.1 %all-gather.5.cloned.1.call-start = ((), (), s32[]{:S(2)}) async-start(), calls=%async_computation | async-start | bytes 8912896 | tf_op jit(solution)/shard_map/all_gather | solution.py:56
  192.2 1.0 copy-start.10
  333.0 6.0 %copy-start = (f32[1024,1024]{0,1:T(8,128)S(1)}, f32[1024,1024]{0,1:T(8,128)}, u32[]{:S(2)}) copy-start(f32[1024,1024]{0,1:T(8,128)} %reshape.140) | copy-start | bytes 12582916
  339.1 7.3 %copy-start.7 = (f32[128,512]{1,0:T(8,128)}, f32[128,512]{1,0:T(8,128)S(1)}, u32[]{:S(2)}) copy-start(f32[128,512]{1,0:T(8,128)S(1)} %fusion.59) | copy-start | bytes 786436
  348.1 1.0 copy-start.9
  495.8 0.7 copy-start.12
  495.8 8.9 %copy-start.4 = (f32[2,8,32,1024]{3,2,1,0:T(8,128)S(1)}, f32[2,8,32,1024]{3,2,1,0:T(8,128)}, u32[]{:S(2)}) copy-start(f32[2,8,32,1024]{3,2,1,0:T(8,128)} %copy.26) | copy-start | bytes 6291460
  500.4 8.9 %copy-start.1 = (f32[2,8,32,1024]{3,2,1,0:T(8,128)S(1)}, f32[2,8,32,1024]{3,2,1,0:T(8,128)}, u32[]{:S(2)}) copy-start(f32[2,8,32,1024]{3,2,1,0:T(8,128)} %copy.27) | copy-start | bytes 6291460
  501.8 11.1 %copy-start.5 = (f32[128,512]{1,0:T(8,128)}, f32[128,512]{1,0:T(8,128)S(1)}, u32[]{:S(2)}) copy-start(f32[128,512]{1,0:T(8,128)S(1)} %fusion.54) | copy-start | bytes 786436
  509.3 3.5 copy-start.2
  517.9 4.0 copy-start.8
  529.1 7.8 %copy-start.6 = (f32[128,512]{1,0:T(8,128)S(1)}, f32[128,512]{1,0:T(8,128)}, u32[]{:S(2)}) copy-start(f32[128,512]{1,0:T(8,128)} %copy-done.5) | copy-start | bytes 786436
  544.0 1.8 copy-start.3
  544.1 2.4 copy-start.11
Sparse Core Ops, SparseCore 0:
  10.3 35.9 all-gather.6
  50.0 66.6 all-gather.8
  118.9 67.6 all-gather.4
where the time goes:
time: 592 us; the launch traced here: 585 us
  other arithmetic  260 us (44%)
  local copies, waits for them, and re-layouts  106 us (18%)
  matrix products  99.3 us (17%)
  waiting for transfers between devices  99.1 us (17%)
  between operations  19.9 us (3%)
    another operation x29, other arithmetic, sym_chol(): return jnp.linalg.cholesky(block)  160 us
    another operation x5, other arithmetic, tri_inverse(): return jax.scipy.linalg.solve_triangular(lower, eye, lower=True)  82.9 us
    all_gather x1, waiting for transfers between devices, local(): blocks = lax.all_gather(corner, ('row', 'col'), axis=0, tiled=True)  65 us
    dot_general x4, matrix products, mm_tn(): lax.dot_general(a, b, (((0,), (0,)), ((), ())), precision=HIGHEST, prefer...  45.8 us
    all_gather x1, waiting for transfers between devices, local(): rows_part = lax.all_gather(kernel[:lead_r, :], 'row', axis=0, tiled=True)  34.1 us
    transpose x1, local copies, waits for them, and re-layouts, local(): a_lead = blocks.transpose(2, 0, 3, 4, 1, 5).reshape(lead, lead)  26.1 us
    dot_general x5, matrix products, mm(): return jnp.dot(a, b, precision=HIGHEST, preferred_element_type=jnp.float32)  25.8 us
    another operation x27, local copies, waits for them, and re-layouts, tri_inverse(): return jax.scipy.linalg.solve_triangular(lower, eye, lower=True)  23.6 us
  transfers between devices with their start and end apart: 3, of which 2 were waited for; matrix products, arithmetic and copies ran while one was open for 69% of the time, Pallas kernels for 0%

commit v1 on v0

--- a/solution.py
+++ b/solution.py
@@ -56,7 +56,11 @@
     cols_part = lax.all_gather(kernel[:, :lead_c], "col", axis=1, tiled=True)
     cols_part = cols_part.reshape(rows_loc, grid_cols, lead_ct, TILE)
     x_rows = cols_part.transpose(0, 2, 1, 3).reshape(rows_loc, lead)
-    rows_part = lax.all_gather(kernel[:lead_r, :], "row", axis=0, tiled=True)
+    block_2 = kernel[:lead_r, :]
+    size = lax.axis_size("row")
+    parts = jnp.stack([block_2 for _ in range(size)])
+    parts = lax.all_to_all(parts, "row", split_axis=0, concat_axis=0)
+    rows_part = jnp.concatenate(parts, axis=0)
     rows_part = rows_part.reshape(grid_rows, lead_rt, TILE, cols_loc)
     y_cols = rows_part.transpose(1, 0, 2, 3).reshape(lead, cols_loc)
     a00 = a_lead[:PANEL, :PANEL]

time: 592 us -> 559 us (0.944)
  waiting for transfers between devices: 99.1 us -> 58.1 us
  starting transfers between devices: 0.12 us -> 6.98 us
    all_gather x1, waiting for transfers between devices: 65 us -> 8.59 us  [local(): blocks = lax.all_gather(corner, ('row', 'col'), axis=0, tiled=True)]
    all_to_all x0 -> x1, waiting for transfers between devices: none -> 49.4 us  [local(): parts = lax.all_to_all(parts, 'row', split_axis=0, concat_axis=0)]
    all_gather x1 -> x0, waiting for transfers between devices: 34.1 us -> none  [local(): rows_part = lax.all_gather(kernel[:lead_r, :], 'row', axis=0, tiled=True)]
    all_to_all x0 -> x1, starting transfers between devices: none -> 6.95 us  [local(): parts = lax.all_to_all(parts, 'row', split_axis=0, concat_axis=0)]
  transfers between devices with their start and end apart: 3 -> 3, of which waited for: 2 -> 2; matrix products, arithmetic and copies ran while one was open for 69% -> 73% of each run, Pallas kernels for 0% -> 0%
where the time goes in v1:
time: 559 us; the launch traced here: 552 us
  other arithmetic  260 us (47%)
  local copies, waits for them, and re-layouts  107 us (19%)
  matrix products  98.8 us (18%)
  waiting for transfers between devices  58.1 us (10%)
  between operations  20.2 us (4%)
  starting transfers between devices  6.98 us (1%)
    another operation x29, other arithmetic, sym_chol(): return jnp.linalg.cholesky(block)  160 us
    another operation x5, other arithmetic, tri_inverse(): return jax.scipy.linalg.solve_triangular(lower, eye, lower=True)  82.9 us
    all_to_all x1, waiting for transfers between devices, local(): parts = lax.all_to_all(parts, 'row', split_axis=0, concat_axis=0)  49.4 us
    dot_general x4, matrix products, mm_tn(): lax.dot_general(a, b, (((0,), (0,)), ((), ())), precision=HIGHEST, prefer...  45.2 us
    transpose x1, local copies, waits for them, and re-layouts, local(): a_lead = blocks.transpose(2, 0, 3, 4, 1, 5).reshape(lead, lead)  26.1 us
    dot_general x5, matrix products, mm(): return jnp.dot(a, b, precision=HIGHEST, preferred_element_type=jnp.float32)  25.8 us
    another operation x27, local copies, waits for them, and re-layouts, tri_inverse(): return jax.scipy.linalg.solve_triangular(lower, eye, lower=True)  23.3 us
    reshape x1, local copies, waits for them, and re-layouts, local(): blocks = blocks.reshape(grid_rows, grid_cols, lead_rt, TILE, lead_ct, TILE)  16.6 us
  transfers between devices with their start and end apart: 3, of which 2 were waited for; matrix products, arithmetic and copies ran while one was open for 73% of the time, Pallas kernels for 0%

profile of v1, /device:TPU:1, one launch (start us, length us, event | category | flops | bytes accessed | tf_op | source)
XLA Modules:
  0.0 552.0 jit_solution(14065870211091037022)
XLA Ops:
  20.7 49.4 %all-to-all-done = f32[8,128,1024]{2,1,0:T(8,128)} async-done(((f32[8,128,1024]{2,1,0:T(8,128)}), f32[8,128,1024]{2,1,0:T(8,128)}, u32[]{:S(2)}, u32[]{:S(2)}) %all-to-all-start) | async-done | bytes 4194336 | tf_op jit(solution)/shard_map/all_to_all | solution.py:62
  84.2 13.2 %reduce.16 = f32[128,8192]{1,0:T(8,128)} reduce(f32[128,1,8192]{2,1,0:T(1,128)} %all-gather.6.cloned.1.call-done, f32[]{:T(128)} %constant.211), dimensions={1}, to_apply=%all-gather.reduce_sub_computation | reduce | bytes 8388612 | tf_op jit(solution)/shard_map/all_gather | solution.py:53
  97.5 16.6 %reshape.138 = f32[8,16,4,32,2,32]{5,4,3,2,1,0:T(2,128)} reshape(f32[128,8192]{1,0:T(8,128)} %reduce.16) | data formatting | bytes 8388608 | tf_op jit(solution)/shard_map/reshape | solution.py:54
  114.1 26.1 %copy.20 = f32[4,8,32,2,16,32]{2,1,0,5,4,3:T(8,128)} copy(f32[4,8,32,2,16,32]{5,3,2,0,4,1:T(2,128)} %bitcast.121) | data formatting | bytes 8388608 | tf_op jit(solution)/shard_map/transpose | solution.py:55
  140.2 14.2 %reshape.139 = f32[1024,1024]{0,1:T(8,128)} reshape(f32[4,8,32,2,16,32]{2,1,0,5,4,3:T(8,128)} %copy.20) | data formatting | bytes 8388608 | tf_op jit(solution)/shard_map/reshape | solution.py:55
  160.7 11.7 %cholesky.286 = f32[128,128]{1,0:T(8,128)S(1)} custom-call(f32[128,128]{1,0:T(8,128)S(1)} %cholesky.426), custom_call_target="Cholesky" | custom-call | tf_op jit(solution)/shard_map/jit(cholesky)/cholesky | solution.py:34
  172.4 9.8 %custom-call.27 = f32[1,128,128]{1,2,0:T(8,128)S(1)} custom-call(f32[1,128,128]{2,1,0:T(8,128)S(1)} %get-tuple-element.61), custom_call_target="InvertDiagBlocksLowerTriangular" | custom-call | tf_op jit(solution)/shard_map/jit(cholesky)/cholesky | solution.py:34
  184.9 11.7 %cholesky.305 = f32[128,128]{1,0:T(8,128)S(1)} custom-call(f32[128,128]{1,0:T(8,128)S(1)} %cholesky.430), custom_call_target="Cholesky" | custom-call | tf_op jit(solution)/shard_map/jit(cholesky)/cholesky | solution.py:34
  196.6 10.0 %custom-call.28 = f32[1,128,128]{1,2,0:T(8,128)S(1)} custom-call(f32[1,128,128]{2,1,0:T(8,128)S(1)} %get-tuple-element.58), custom_call_target="InvertDiagBlocksLowerTriangular" | custom-call | tf_op jit(solution)/shard_map/jit(cholesky)/cholesky | solution.py:34
  208.2 11.7 %cholesky.326 = f32[128,128]{1,0:T(8,128)S(1)} custom-call(f32[128,128]{1,0:T(8,128)S(1)} %cholesky.435), custom_call_target="Cholesky" | custom-call | tf_op jit(solution)/shard_map/jit(cholesky)/cholesky | solution.py:34
  219.9 9.8 %custom-call.29 = f32[1,128,128]{1,2,0:T(8,128)S(1)} custom-call(f32[1,128,128]{2,1,0:T(8,128)S(1)} %get-tuple-element.55), custom_call_target="InvertDiagBlocksLowerTriangular" | custom-call | tf_op jit(solution)/shard_map/jit(cholesky)/cholesky | solution.py:34
  231.2 11.7 %cholesky.343 = f32[128,128]{1,0:T(8,128)S(1)} custom-call(f32[128,128]{1,0:T(8,128)S(1)} %convolution_subtract_fusion.12), custom_call_target="Cholesky" | custom-call | tf_op jit(solution)/shard_map/jit(cholesky)/cholesky | solution.py:34
  249.3 11.7 %while.4 = (s32[]{:T(128)}, f32[512,512]{1,0:T(8,128)}, s32[4,2]{0,1:T(2,128)S(1)}, f32[4,128,128]{2,1,0:T(8,128)S(1)}, s32[]{:T(128)}) while((s32[]{:T(128)}, f32[512,512]{1,0:T(8,128)}, s32[4,2]{0,1:T(2,128)S(1)}, f32[4,128,128]{2,1,0:T(8,128)S(1)}, s32[]{:T(128)}) %tuple.58), condition=%wide.while_cond, body=%wide.while_body.sunk | while | flops 2 | bytes 131181 | solution.py:30
  261.0 39.3 %custom-call.30 = f32[4,128,128]{1,2,0:T(8,128)S(1)} custom-call(f32[4,128,128]{2,1,0:T(8,128)S(1)} %get-tuple-element.18), custom_call_target="InvertDiagBlocksLowerTriangular" | custom-call | tf_op jit(solution)/shard_map/jit(_solve_triangular)/triangular_solve | solution.py:30
  316.5 11.7 %cholesky.358 = f32[128,128]{1,0:T(8,128)S(1)} custom-call(f32[128,128]{1,0:T(8,128)S(1)} %cholesky.439), custom_call_target="Cholesky" | custom-call | tf_op jit(solution)/shard_map/jit(cholesky)/cholesky | solution.py:34
  329.3 10.0 %custom-call.31 = f32[1,128,128]{1,2,0:T(8,128)S(1)} custom-call(f32[1,128,128]{2,1,0:T(8,128)S(1)} %get-tuple-element.51), custom_call_target="InvertDiagBlocksLowerTriangular" | custom-call | tf_op jit(solution)/shard_map/jit(cholesky)/cholesky | solution.py:34
  342.5 11.7 %cholesky.377 = f32[128,128]{1,0:T(8,128)S(1)} custom-call(f32[128,128]{1,0:T(8,128)S(1)} %cholesky.443), custom_call_target="Cholesky" | custom-call | tf_op jit(solution)/shard_map/jit(cholesky)/cholesky | solution.py:34
  354.8 9.8 %custom-call.32 = f32[1,128,128]{1,2,0:T(8,128)S(1)} custom-call(f32[1,128,128]{2,1,0:T(8,128)S(1)} %get-tuple-element.48), custom_call_target="InvertDiagBlocksLowerTriangular" | custom-call | tf_op jit(solution)/shard_map/jit(cholesky)/cholesky | solution.py:34
  367.0 11.7 %cholesky.398 = f32[128,128]{1,0:T(8,128)S(1)} custom-call(f32[128,128]{1,0:T(8,128)S(1)} %cholesky.448), custom_call_target="Cholesky" | custom-call | tf_op jit(solution)/shard_map/jit(cholesky)/cholesky | solution.py:34
  379.3 10.0 %custom-call.33 = f32[1,128,128]{1,2,0:T(8,128)S(1)} custom-call(f32[1,128,128]{2,1,0:T(8,128)S(1)} %get-tuple-element.45), custom_call_target="InvertDiagBlocksLowerTriangular" | custom-call | tf_op jit(solution)/shard_map/jit(cholesky)/cholesky | solution.py:34
  391.6 11.7 %cholesky.415 = f32[128,128]{1,0:T(8,128)S(1)} custom-call(f32[128,128]{1,0:T(8,128)S(1)} %convolution_subtract_fusion.11), custom_call_target="Cholesky" | custom-call | tf_op jit(solution)/shard_map/jit(cholesky)/cholesky | solution.py:34
  411.7 11.7 %while.5 = (s32[]{:T(128)}, f32[512,512]{1,0:T(8,128)}, s32[4,2]{0,1:T(2,128)S(1)}, f32[4,128,128]{2,1,0:T(8,128)S(1)}, s32[]{:T(128)}) while((s32[]{:T(128)}, f32[512,512]{1,0:T(8,128)}, s32[4,2]{0,1:T(2,128)S(1)}, f32[4,128,128]{2,1,0:T(8,128)S(1)}, s32[]{:T(128)}) %tuple.68), condition=%wide.while_cond.clone, body=%wide.while_body.clone.sunk | while | flops 2 | bytes 131181 | solution.py:30
  423.4 39.7 %custom-call.34 = f32[4,128,128]{1,2,0:T(8,128)S(1)} custom-call(f32[4,128,128]{2,1,0:T(8,128)S(1)} %get-tuple-element.19), custom_call_target="InvertDiagBlocksLowerTriangular" | custom-call | tf_op jit(solution)/shard_map/jit(_solve_triangular)/triangular_solve | solution.py:30
  513.2 31.7 %subtract_select_fusion = f32[2048,1024]{1,0:T(8,128)} fusion(f32[2048,1024]{1,0:T(8,128)} %param.4, pred[1024]{0:T(1024)(128)(4,1)S(1)} %get-tuple-element.67, pred[2048]{0:T(1024)(128)(4,1)S(1)} %get-tuple-element.69, f32[512,1024]{1,0:T(8,128)S(1)} %copy-done.11, f32[512,1024]{1,0:T(8,128)S(1)} %copy-done.3, f32[512,2048]{1,0:T(8,128)S(1)} %fusion.7, ...), kind=kOutput, calls=%fused_computation.8 | convolution fusion | flops 25779240960 | bytes 29363200 | tf_op jit(solution)/shard_map/dot_general | solution.py:17
  (140 shorter events, 148.4 us)
Async XLA Ops:
  7.2 77.1 %all-gather.6.cloned.1.call-start = ((), (), s32[]{:S(2)}) async-start(), calls=%async_computation.2 | async-start | bytes 4227072 | tf_op jit(solution)/shard_map/all_gather | solution.py:53
  12.4 7.0 %slice-start = ((f32[2048,1024]{1,0:T(8,128)}), f32[2048,64]{1,0:T(8,128)S(1)}, s32[]{:S(2)}) async-start(f32[2048,1024]{1,0:T(8,128)} %param.4), calls=%async_computation.3 | async-start | bytes 2097152 | tf_op jit(solution)/shard_map/slice | solution.py:56
  12.4 57.7 %all-to-all-start = ((f32[8,128,1024]{2,1,0:T(8,128)}), f32[8,128,1024]{2,1,0:T(8,128)}, u32[]{:S(2)}, u32[]{:S(2)}) async-start(f32[8,128,1024]{2,1,0:T(8,128)} %stack.2), calls=%async_computation | async-start | bytes 8388608 | tf_op jit(solution)/shard_map/all_to_all | solution.py:62
  19.4 465.9 %all-gather.4.cloned.1.call-start = ((), (), s32[]{:S(2)}) async-start(), calls=%async_computation.1 | async-start | bytes 8912896 | tf_op jit(solution)/shard_map/all_gather | solution.py:56
  159.7 1.0 copy-start.10
  300.3 6.1 %copy-start = (f32[1024,1024]{0,1:T(8,128)S(1)}, f32[1024,1024]{0,1:T(8,128)}, u32[]{:S(2)}) copy-start(f32[1024,1024]{0,1:T(8,128)} %reshape.139) | copy-start | bytes 12582916
  306.4 7.3 %copy-start.7 = (f32[128,512]{1,0:T(8,128)}, f32[128,512]{1,0:T(8,128)S(1)}, u32[]{:S(2)}) copy-start(f32[128,512]{1,0:T(8,128)S(1)} %fusion.59) | copy-start | bytes 786436
  315.5 1.0 copy-start.9
  463.1 0.7 copy-start.12
  463.2 8.9 %copy-start.4 = (f32[2,8,32,1024]{3,2,1,0:T(8,128)S(1)}, f32[2,8,32,1024]{3,2,1,0:T(8,128)}, u32[]{:S(2)}) copy-start(f32[2,8,32,1024]{3,2,1,0:T(8,128)} %copy.26) | copy-start | bytes 6291460
  467.7 8.9 %copy-start.1 = (f32[2,8,32,1024]{3,2,1,0:T(8,128)S(1)}, f32[2,8,32,1024]{3,2,1,0:T(8,128)}, u32[]{:S(2)}) copy-start(f32[2,8,32,1024]{3,2,1,0:T(8,128)} %copy.27) | copy-start | bytes 6291460
  469.1 11.1 %copy-start.5 = (f32[128,512]{1,0:T(8,128)}, f32[128,512]{1,0:T(8,128)S(1)}, u32[]{:S(2)}) copy-start(f32[128,512]{1,0:T(8,128)S(1)} %fusion.54) | copy-start | bytes 786436
  476.6 3.5 copy-start.2
  485.2 4.0 copy-start.8
  496.4 7.2 %copy-start.6 = (f32[128,512]{1,0:T(8,128)S(1)}, f32[128,512]{1,0:T(8,128)}, u32[]{:S(2)}) copy-start(f32[128,512]{1,0:T(8,128)} %copy-done.5) | copy-start | bytes 786436
  510.8 1.8 copy-start.3
  510.8 2.4 copy-start.11
Sparse Core Ops, SparseCore 0:
  11.1 73.0 all-gather.5
  87.0 67.5 all-gather.3
